TPU v7x, 256 devices: a whole 4x4x8 slice. The times are simulated.
256 devices in a mesh: grp: 128 (over z, x, y), rep: 2 (over core).
Axes of the slice: x: 4, y: 4, z: 8, core: 2. Of those that a mesh axis runs over, the one named last changes fastest.
Arguments:
- snapshots: float32 [128, 2048, 1024], P('grp', 'rep'), may hold values from -6 to 6
- row_factor: float32 [2048, 128], P('rep'), may hold values from -0.125 to 0.125
- time_factor: float32 [128, 64], replicated, may hold values from -0.5 to 0.5
Outputs:
- new_rows: float32 [2048, 128], P('rep')
- new_time: float32 [128, 64], replicated
All inputs are finite; a program needn't handle non-finite values.
Results may differ from a plain program's by a relative error of at most 0.0001.
Values sent between devices are 32-bit elements; how exact they have to be, the bound alone decides.
A program may use at most 64 MiB of HBM per device.

v0:
```python
import math
import jax
import jax.numpy as jnp
from jax import lax
from jax.sharding import PartitionSpec as P

ROWS = 2048
STEPS = 8


def highdot(left, right):
    return jnp.dot(left, right, precision=lax.Precision.HIGHEST, preferred_element_type=jnp.float32)


def orthogonalize(start_matrix):
    total = jnp.sum(start_matrix * start_matrix)
    iterate = start_matrix / jnp.sqrt(total + 1e-06)
    for step_index in range(STEPS):
        inner = highdot(iterate.T, iterate)
        iterate = 1.5 * iterate - 0.5 * highdot(iterate, inner)
    return iterate


def on_device(snapshots, row_factor, time_factor):
    row_half = snapshots.shape[1]
    rank_row = row_factor.shape[1]
    projected = jnp.einsum("tij,ia->tja", snapshots, row_factor, precision=lax.Precision.HIGHEST)
    summed = lax.psum(projected, "rep")
    owned = lax.all_to_all(summed, "grp", split_axis=1, concat_axis=0, tiled=True)
    snaps = owned.shape[0]
    width = owned.shape[1] * rank_row
    flat = owned.reshape(snaps, width)
    halfwidth = width // 2
    portion = lax.dynamic_slice_in_dim(flat, lax.axis_index("rep") * halfwidth, halfwidth, 1)
    gram_part = highdot(portion, portion.T)
    gram_total = lax.psum(gram_part, ("grp", "rep"))
    start_time = highdot(gram_total, time_factor)
    basis_time = orthogonalize(start_time)
    mixer = highdot(basis_time, basis_time.T)
    weights = highdot(mixer, flat).reshape(owned.shape)
    returned = lax.all_to_all(weights, "grp", split_axis=0, concat_axis=1, tiled=True)
    own_rows = lax.psum_scatter(
        jnp.einsum("tij,tja->ia", snapshots, returned, precision=lax.Precision.HIGHEST),
        "grp",
        scatter_dimension=0,
        tiled=True,
    )
    half_block = lax.all_gather(own_rows, "grp", axis=0, tiled=True)
    all_block = lax.all_gather(half_block, "rep", axis=0, tiled=True)
    basis = orthogonalize(all_block)
    new_rows = lax.dynamic_slice_in_dim(basis, lax.axis_index("rep") * row_half, row_half, 0)
    return (new_rows * math.sqrt(ROWS), basis_time * math.sqrt(snaps))


def solution(mesh):
    return jax.shard_map(
        on_device,
        mesh=mesh,
        in_specs=(P("grp", "rep", None), P("rep", None), P()),
        out_specs=(P("rep", None), P()),
        check_vma=False,
    )
```

profile of v0, /device:TPU:1, one launch (start us, length us, event | category | flops | bytes accessed | tf_op | source)
XLA Modules:
  0.0 982.5 jit_solution(4008514134810224522)
XLA Ops:
  7.2 1.0 copy-done
  8.2 9.6 fusion.11
  17.9 34.2 %all-reduce.5.cloned.1.call-done = f32[1,1024,128]{2,1,0:T(8,128)} async-done(((f32[1,1024,128]{2,1,0:T(8,128)}), f32[1,1024,128]{2,1,0:T(8,128)}) %all-reduce.5.cloned.1.call-update) | async-done | bytes 524304 | tf_op jit(solution)/shard_map/psum | solution.py:28
  52.1 13.6 %all-to-all-start = ((f32[1,1024,128]{2,0,1:T(1,128)}), f32[1,1024,128]{2,0,1:T(1,128)S(1)}, u32[]{:S(2)}, u32[]{:S(2)}) async-start(f32[1,1024,128]{2,0,1:T(1,128)} %bitcast.92), calls=%async_computation | async-start | bytes 1048576 | tf_op jit(solution)/shard_map/all_to_all | solution.py:29
  65.7 19.0 %all-to-all-done = f32[1,1024,128]{2,0,1:T(1,128)S(1)} async-done(((f32[1,1024,128]{2,0,1:T(1,128)}), f32[1,1024,128]{2,0,1:T(1,128)S(1)}, u32[]{:S(2)}, u32[]{:S(2)}) %all-to-all-start) | async-done | bytes 524320 | tf_op jit(solution)/shard_map/all_to_all | solution.py:29
  85.2 1.9 reduce.3
  87.1 1.0 fusion.29
  88.9 231.8 %all-reduce.7.cloned.1.call-done = f32[128,128]{1,0:T(8,128)} async-done(((f32[128,128]{1,0:T(8,128)}), f32[128,128]{1,0:T(8,128)}) %all-reduce.7.cloned.1.call-update) | async-done | bytes 65552 | tf_op jit(solution)/shard_map/psum | solution.py:36
  320.7 1.7 multiply_reduce_fusion.1
  328.4 25.9 %all_to_all.8 = f32[128,8,128]{2,1,0:T(8,128)S(1)} all-to-all(f32[128,8,128]{2,1,0:T(8,128)S(1)} %copy.28), channel_id=1, replica_groups=mesh['grp'=128,'rep'=2] {'grp'}, dimensions={0} | all-to-all | bytes 1048576 | tf_op jit(solution)/shard_map/all_to_all | solution.py:41
  354.3 5.4 fusion.14
  360.9 206.4 %all-reduce.9.cloned.1.call-done = f32[1024,128]{0,1:T(8,128)} async-done(((f32[1024,128]{0,1:T(8,128)}), f32[1024,128]{0,1:T(8,128)}) %all-reduce.9.cloned.1.call-update) | async-done | bytes 524304
  568.3 309.8 %all_gather.6 = f32[1024,128]{1,0:T(8,128)} all-gather(f32[8,128]{1,0:T(8,128)S(1)} %copy.29), channel_id=1, replica_groups=mesh['grp'=128,'rep'=2] {'grp'}, dimensions={0}, use_global_device_ids=true | all-gather | bytes 528384 | tf_op jit(solution)/shard_map/all_gather | solution.py:48
  878.2 69.5 %all-gather.2.cloned.1.call-done = f32[2048,128]{1,0:T(8,128)} async-done(((f32[1024,128]{1,0:T(8,128)}), f32[2048,128]{1,0:T(8,128)}) %all-gather.2.cloned.1.call-update) | async-done | bytes 1048592 | tf_op jit(solution)/shard_map/all_gather | solution.py:49
  947.7 2.2 multiply_reduce_fusion
  950.6 3.4 fusion.28
  955.0 1.8 fusion.41
  957.8 1.8 fusion.42
  960.6 1.8 fusion.43
  962.4 1.2 fusion.7
  963.6 1.8 fusion.44
  966.4 1.8 fusion.45
  969.2 1.8 fusion.46
  972.0 1.8 fusion.47
  (50 shorter events, 15.9 us)
Async XLA Ops:
  7.2 1.0 copy-start
  7.2 313.5 %copy-start.3 = (f32[128,64]{0,1:T(8,128)S(1)}, f32[128,64]{0,1:T(8,128)}, u32[]{:S(2)}) copy-start(f32[128,64]{0,1:T(8,128)} %param.5) | copy-start | bytes 98308
  7.2 44.9 %all-reduce.5.cloned.1.call-start = ((), (), s32[]{:S(2)}) async-start(), calls=%async_computation.2 | async-start | bytes 1048576 | tf_op jit(solution)/shard_map/psum | solution.py:28
  52.1 32.6 %all-to-all-start = ((f32[1,1024,128]{2,0,1:T(1,128)}), f32[1,1024,128]{2,0,1:T(1,128)S(1)}, u32[]{:S(2)}, u32[]{:S(2)}) async-start(f32[1,1024,128]{2,0,1:T(1,128)} %bitcast.92), calls=%async_computation | async-start | bytes 1048576 | tf_op jit(solution)/shard_map/all_to_all | solution.py:29
  65.6 255.1 %all-reduce.7.cloned.1.call-start = ((), (), s32[]{:S(2)}) async-start(), calls=%async_computation.3 | async-start | bytes 131072 | tf_op jit(solution)/shard_map/psum | solution.py:36
  88.2 479.2 %all-reduce.9.cloned.1.call-start = ((), (), s32[]{:S(2)}) async-start(), calls=%async_computation.5 | async-start | bytes 1048576
  323.1 31.2 %copy-start.1 = (f32[1,1024,1024]{2,1,0:T(8,128)S(1)}, f32[1,1024,1024]{2,1,0:T(8,128)}, u32[]{:S(2)}) copy-start(f32[1,1024,1024]{2,1,0:T(8,128)} %param.3) | copy-start | bytes 12582916
  328.1 31.7 %copy-start.4 = (u32[256]{0:T(256)S(1)}, u32[256]{0:T(256)}, u32[]{:S(2)}) copy-start(u32[256]{0:T(256)} %constant.29) | copy-start | bytes 3076
  359.7 588.0 %all-gather.2.cloned.1.call-start = ((), (), s32[]{:S(2)}) async-start(), calls=%async_computation.4 | async-start | bytes 1572864 | tf_op jit(solution)/shard_map/all_gather | solution.py:49
  947.7 6.3 copy-start.2
Sparse Core Ops, SparseCore 0:
  18.0 34.0 all-reduce.4
  88.3 232.3 all-reduce.6
  359.8 207.4 all-reduce.8
  878.3 69.3 all-gather.1
where the time goes:
time: 990 us; the launch traced here: 982 us
  waiting for transfers between devices  561 us (57%)
  blocking collectives  336 us (34%)
  matrix products  46.7 us (5%)
  between operations  16.3 us (2%)
  starting transfers between devices  14.2 us (1%)
    all_gather x1, blocking collectives, on_device(): half_block = lax.all_gather(own_rows, 'grp', axis=0, tiled=True)  310 us
    psum x1, waiting for transfers between devices, on_device(): gram_total = lax.psum(gram_part, ('grp', 'rep'))  232 us
    unnamed x5, waiting for transfers between devices  206 us
    all_gather x1, waiting for transfers between devices, on_device(): all_block = lax.all_gather(half_block, 'rep', axis=0, tiled=True)  69.5 us
    psum x1, waiting for transfers between devices, on_device(): summed = lax.psum(projected, 'rep')  34.2 us
    dot_general x36, matrix products, highdot(): jnp.dot(left, right, precision=lax.Precision.HIGHEST, preferred_element_t...  31.7 us
    all_to_all x1, blocking collectives, on_device(): lax.all_to_all(weights, 'grp', split_axis=0, concat_axis=1, tiled=True)  25.9 us
  transfers between devices with their start and end apart: 5, of which 5 were waited for; matrix products, arithmetic and copies ran while one was open for 0% of the time, Pallas kernels for 0%

commit v1 on v0

--- a/solution.py
+++ b/solution.py
@@ -6,6 +6,11 @@
 
 ROWS = 2048
 STEPS = 8
+
+
+def add_all(array, axis):
+    pieces = lax.all_gather(array, axis)
+    return jnp.sum(pieces, axis=0)
 
 
 def highdot(left, right):
@@ -33,7 +38,7 @@
     halfwidth = width // 2
     portion = lax.dynamic_slice_in_dim(flat, lax.axis_index("rep") * halfwidth, halfwidth, 1)
     gram_part = highdot(portion, portion.T)
-    gram_total = lax.psum(gram_part, ("grp", "rep"))
+    gram_total = add_all(gram_part, ("grp", "rep"))
     start_time = highdot(gram_total, time_factor)
     basis_time = orthogonalize(start_time)
     mixer = highdot(basis_time, basis_time.T)

time: 990 us -> 885 us (0.89)
  waiting for transfers between devices: 561 us -> 447 us
    psum x1 -> x0, waiting for transfers between devices: 232 us -> none  [on_device(): gram_total = lax.psum(gram_part, ('grp', 'rep'))]
    all_gather x0 -> x1, waiting for transfers between devices: none -> 119 us  [add_all(): pieces = lax.all_gather(array, axis)]
where the time goes in v1:
time: 885 us; the launch traced here: 877 us
  waiting for transfers between devices  447 us (51%)
  blocking collectives  338 us (38%)
  matrix products  45.9 us (5%)
  between operations  16.3 us (2%)
  starting transfers between devices  14.2 us (2%)
  other arithmetic  11.6 us (1%)
    all_gather x1, blocking collectives, on_device(): half_block = lax.all_gather(own_rows, 'grp', axis=0, tiled=True)  310 us
    unnamed x5, waiting for transfers between devices  205 us
    all_gather x1, waiting for transfers between devices, add_all(): pieces = lax.all_gather(array, axis)  119 us
    all_gather x1, waiting for transfers between devices, on_device(): all_block = lax.all_gather(half_block, 'rep', axis=0, tiled=True)  69.5 us
    psum x1, waiting for transfers between devices, on_device(): summed = lax.psum(projected, 'rep')  34.2 us
    dot_general x36, matrix products, highdot(): jnp.dot(left, right, precision=lax.Precision.HIGHEST, preferred_element_t...  30.9 us
    all_to_all x1, blocking collectives, on_device(): lax.all_to_all(weights, 'grp', split_axis=0, concat_axis=1, tiled=True)  28.5 us
    all_to_all x1, waiting for transfers between devices, on_device(): lax.all_to_all(summed, 'grp', split_axis=1, concat_axis=0, tiled=True)  19 us
  transfers between devices with their start and end apart: 5, of which 5 were waited for; matrix products, arithmetic and copies ran while one was open for 0% of the time, Pallas kernels for 0%

profile of v1, /device:TPU:1, one launch (start us, length us, event | category | flops | bytes accessed | tf_op | source)
XLA Modules:
  0.0 877.1 jit_solution(12701275597162375894)
XLA Ops:
  7.2 1.0 copy-done
  8.2 9.6 %fusion.11 = f32[1,1024,128]{2,1,0:T(8,128)} fusion(f32[1024,128]{1,0:T(8,128)S(1)} %copy-done, f32[1,1024,1024]{2,1,0:T(8,128)} %param.3), kind=kOutput, calls=%fused_computation.18 | convolution fusion | flops 1610612736 | bytes 5242880 | tf_op jit(solution)/shard_map/tij,ia->tja/dot_general | solution.py:32
  17.9 34.2 %all-reduce.4.cloned.1.call-done = f32[1,1024,128]{2,1,0:T(8,128)} async-done(((f32[1,1024,128]{2,1,0:T(8,128)}), f32[1,1024,128]{2,1,0:T(8,128)}) %all-reduce.4.cloned.1.call-update) | async-done | bytes 524304 | tf_op jit(solution)/shard_map/psum | solution.py:33
  52.1 13.6 %all-to-all-start = ((f32[1,1024,128]{2,0,1:T(1,128)}), f32[1,1024,128]{2,0,1:T(1,128)S(1)}, u32[]{:S(2)}, u32[]{:S(2)}) async-start(f32[1,1024,128]{2,0,1:T(1,128)} %bitcast.94), calls=%async_computation | async-start | bytes 1048576 | tf_op jit(solution)/shard_map/all_to_all | solution.py:34
  65.7 19.0 %all-to-all-done = f32[1,1024,128]{2,0,1:T(1,128)S(1)} async-done(((f32[1,1024,128]{2,0,1:T(1,128)}), f32[1,1024,128]{2,0,1:T(1,128)S(1)}, u32[]{:S(2)}, u32[]{:S(2)}) %all-to-all-start) | async-done | bytes 524320 | tf_op jit(solution)/shard_map/all_to_all | solution.py:34
  85.2 1.9 reduce.3
  87.1 1.0 fusion.29
  88.9 119.2 %all-gather.6.cloned.1.call-done = f32[32768,128]{1,0:T(8,128)} async-done(((f32[128,128]{1,0:T(8,128)}), f32[32768,128]{1,0:T(8,128)}) %all-gather.6.cloned.1.call-update) | async-done | bytes 16777232 | tf_op jit(solution)/shard_map/all_gather | solution.py:12
  208.1 6.6 reduce_sum.27
  221.6 28.5 %all_to_all.8 = f32[128,8,128]{2,1,0:T(8,128)S(1)} all-to-all(f32[128,8,128]{2,1,0:T(8,128)S(1)} %copy.28), channel_id=1, replica_groups=mesh['grp'=128,'rep'=2] {'grp'}, dimensions={0} | all-to-all | bytes 1048576 | tf_op jit(solution)/shard_map/all_to_all | solution.py:46
  250.2 5.4 fusion.14
  256.7 205.2 %all-reduce.6.cloned.1.call-done = f32[1024,128]{0,1:T(8,128)} async-done(((f32[1024,128]{0,1:T(8,128)}), f32[1024,128]{0,1:T(8,128)}) %all-reduce.6.cloned.1.call-update) | async-done | bytes 524304
  462.9 309.8 %all_gather.14 = f32[1024,128]{1,0:T(8,128)} all-gather(f32[8,128]{1,0:T(8,128)S(1)} %copy.29), channel_id=1, replica_groups=mesh['grp'=128,'rep'=2] {'grp'}, dimensions={0}, use_global_device_ids=true | all-gather | bytes 528384 | tf_op jit(solution)/shard_map/all_gather | solution.py:53
  772.8 69.5 %all-gather.4.cloned.1.call-done = f32[2048,128]{1,0:T(8,128)} async-done(((f32[1024,128]{1,0:T(8,128)}), f32[2048,128]{1,0:T(8,128)}) %all-gather.4.cloned.1.call-update) | async-done | bytes 1048592 | tf_op jit(solution)/shard_map/all_gather | solution.py:54
  842.3 2.2 multiply_reduce_fusion
  845.2 3.4 fusion.28
  849.6 1.8 fusion.41
  852.4 1.8 fusion.42
  855.2 1.8 fusion.43
  857.0 1.2 fusion.7
  858.2 1.8 fusion.44
  861.0 1.8 fusion.45
  863.8 1.8 fusion.46
  866.6 1.8 fusion.47
  (51 shorter events, 16.7 us)
Async XLA Ops:
  7.2 1.0 copy-start
  7.2 44.9 %all-reduce.4.cloned.1.call-start = ((), (), s32[]{:S(2)}) async-start(), calls=%async_computation.2 | async-start | bytes 1048576 | tf_op jit(solution)/shard_map/psum | solution.py:33
  52.1 32.6 %all-to-all-start = ((f32[1,1024,128]{2,0,1:T(1,128)}), f32[1,1024,128]{2,0,1:T(1,128)S(1)}, u32[]{:S(2)}, u32[]{:S(2)}) async-start(f32[1,1024,128]{2,0,1:T(1,128)} %bitcast.94), calls=%async_computation | async-start | bytes 1048576 | tf_op jit(solution)/shard_map/all_to_all | solution.py:34
  65.6 142.5 %all-gather.6.cloned.1.call-start = ((), (), s32[]{:S(2)}) async-start(), calls=%async_computation.4 | async-start | bytes 16842752 | tf_op jit(solution)/shard_map/all_gather | solution.py:12
  88.2 373.8 %all-reduce.6.cloned.1.call-start = ((), (), s32[]{:S(2)}) async-start(), calls=%async_computation.5 | async-start | bytes 1048576
  208.1 6.6 copy-start.3
  216.3 33.9 %copy-start.1 = (f32[1,1024,1024]{2,1,0:T(8,128)S(1)}, f32[1,1024,1024]{2,1,0:T(8,128)}, u32[]{:S(2)}) copy-start(f32[1,1024,1024]{2,1,0:T(8,128)} %param.3) | copy-start | bytes 12582916
  221.3 34.3 %copy-start.4 = (u32[256]{0:T(256)S(1)}, u32[256]{0:T(256)}, u32[]{:S(2)}) copy-start(u32[256]{0:T(256)} %constant.29) | copy-start | bytes 3076
  255.5 586.8 %all-gather.4.cloned.1.call-start = ((), (), s32[]{:S(2)}) async-start(), calls=%async_computation.3 | async-start | bytes 1572864 | tf_op jit(solution)/shard_map/all_gather | solution.py:54
  842.3 6.3 copy-start.2
Sparse Core Ops, SparseCore 0:
  18.0 34.0 all-reduce.3
  88.3 119.7 all-gather.5
  255.7 206.2 all-reduce.5
  772.9 69.3 all-gather.3
